TPU v7x, 512 devices: a whole 4x8x8 slice. The times are simulated.
512 devices in a mesh: feat: 128 (over y, x, z_lo, core), layer: 4 (over z_hi).
Axes of the slice: x: 4, y: 8, z: 8 (z_hi: 4, z_lo: 2; z = z_hi * 2 + z_lo), core: 2. Of those that a mesh axis runs over, the one named last changes fastest.
Arguments:
- residual_in: bfloat16 [4, 384, 2304], P('layer', 'feat'), as said below
- enc_weight: bfloat16 [4, 2304, 8192], P('layer', None, 'feat'), as said below
- thresholds: int32 [4, 8192], P('layer', 'feat'), may hold values from -2016 to 7341, as said below
- dec_weight: bfloat16 [4, 4, 8192, 2304], P(None, 'layer', 'feat'), may hold values from -0.03125 to 0.03125
- target: bfloat16 [4, 384, 2304], P('layer', 'feat')
Outputs:
- loss_value: float32 [], replicated
- reconstruction: bfloat16 [4, 384, 2304], P('layer', 'feat')
- dec_grad: bfloat16 [4, 4, 8192, 2304], P(None, 'layer', 'feat')
- enc_grad: bfloat16 [4, 2304, 8192], P('layer', None, 'feat')
Inputs may be any that keep to these rules, and one draw needn't show every extreme that they name: `residual_in`: every entry is a multiple of 1/8. `enc_weight`: every entry is a multiple of 1/256. `thresholds`: whole numbers.
All inputs are finite; a program needn't handle non-finite values.
Results may differ from a plain program's by a relative error of at most 0.007.
Values may be sent and summed in bfloat16 or wider, within the bound.
A program may use at most 64 MiB of HBM per device.

v0:
```python
import jax
import jax.numpy as jnp
from jax import lax
from jax.sharding import PartitionSpec as P

ERROR_SCALE = 32.0
PENALTY_WEIGHT = 4.0


def body(residual_in, enc_weight, thresholds, dec_weight, target):
    local_rows = residual_in[0]
    encoder = enc_weight[0]
    jump_level = (thresholds[0].astype(jnp.float32) + 0.5) / 2048.0
    preactivation = jnp.dot(
        lax.all_gather(local_rows, "feat", axis=0, tiled=True),
        encoder,
        preferred_element_type=jnp.float32,
    )
    active_mask = preactivation > jump_level[None, :]
    layer_activations = jnp.where(active_mask, preactivation, 0.0).astype(jnp.bfloat16)
    token_count = preactivation.shape[0]
    magnitude = jnp.mean(jnp.abs(layer_activations.astype(jnp.float32)), axis=0)
    penalty_local = jnp.sum(magnitude * magnitude)
    penalty_total = lax.psum(penalty_local, ("feat", "layer"))
    all_acts = lax.all_gather(layer_activations[None], "layer", axis=0, tiled=True)
    decoder = dec_weight[:, 0]
    recon = lax.psum_scatter(
        jnp.einsum("sif,sfd->id", all_acts, decoder, preferred_element_type=jnp.float32),
        "feat",
        scatter_dimension=0,
        tiled=True,
    )
    error_rows = recon - target[0].astype(jnp.float32)
    grad_local = (error_rows / ERROR_SCALE).astype(jnp.bfloat16)
    grad_all = lax.all_gather(grad_local, "feat", axis=0, tiled=True)
    squares_local = jnp.sum(error_rows * error_rows)
    squares_total = lax.psum(squares_local, ("feat", "layer"))
    dec_grad = jnp.einsum(
        "sif,id->sfd", all_acts, grad_all, preferred_element_type=jnp.float32
    ).astype(jnp.bfloat16)
    act_part = jnp.einsum("id,sfd->sif", grad_all, decoder, preferred_element_type=jnp.float32)
    activation_gradient = lax.psum_scatter(act_part, "layer", scatter_dimension=0, tiled=True)[0]
    sparsity_gradient = (
        2.0
        * PENALTY_WEIGHT
        * magnitude[None, :]
        * jnp.sign(layer_activations.astype(jnp.float32))
        / token_count
    )
    preactivation_gradient = jnp.where(
        active_mask, activation_gradient + sparsity_gradient, 0.0
    ).astype(jnp.bfloat16)
    enc_grad = jnp.einsum(
        "id,if->df",
        lax.all_gather(local_rows, "feat", axis=0, tiled=True),
        preactivation_gradient,
        preferred_element_type=jnp.float32,
    )
    loss_value = (squares_total + 2.0 * ERROR_SCALE * PENALTY_WEIGHT * penalty_total) / (
        lax.axis_size("layer") * token_count * local_rows.shape[1]
    )
    return (
        loss_value,
        recon.astype(jnp.bfloat16)[None],
        dec_grad[:, None],
        enc_grad.astype(jnp.bfloat16)[None],
    )


def solution(mesh):
    return jax.shard_map(
        body,
        mesh=mesh,
        in_specs=(
            P("layer", "feat", None),
            P("layer", None, "feat"),
            P("layer", "feat"),
            P(None, "layer", "feat", None),
            P("layer", "feat", None),
        ),
        out_specs=(
            P(),
            P("layer", "feat", None),
            P(None, "layer", "feat", None),
            P("layer", None, "feat"),
        ),
        check_vma=False,
    )
```

profile of v0, /device:TPU:1, one launch (start us, length us, event | category | flops | bytes accessed | tf_op | source)
XLA Modules:
  0.0 1679.2 jit_solution(8954540019723485133)
XLA Ops:
  7.2 0.0 copy-start
  7.2 0.0 all-gather.6.cloned.1.call-start
  7.2 1.4 copy.19
  8.7 0.0 all-gather.6.cloned.1.call-update
  8.7 0.0 all-reduce.4.cloned.1.call-start
  8.7 0.7 multiply_bitcast_fusion
  9.4 223.4 %all-gather.6.cloned.1.call-done = bf16[1,384,2304]{2,0,1:T(2,128)(2,1)} async-done(((bf16[1,3,2304]{2,0,1:T(2,128)(2,1)}), bf16[1,384,2304]{2,0,1:T(2,128)(2,1)}) %all-gather.6.cloned.1.call-update) | async-done | bytes 1769488 | tf_op jit(solution)/shard_map/all_gather | solution.py:15
  232.8 2.8 fusion.14
  235.6 14.4 all-gather.1
  250.1 0.0 copy-done
  250.1 2.5 convolution_bitcast_fusion
  252.6 0.0 copy-start.1
  252.6 0.0 all-reduce.4.cloned.1.call-update
  252.6 0.0 all-gather.8.cloned.1.call-start
  252.6 1.3 dynamic-slice
  254.6 1085.1 %all-reduce.4.cloned.1.call-done = f32[384,2304]{1,0:T(8,128)} async-done(((f32[384,2304]{1,0:T(8,128)}), f32[384,2304]{1,0:T(8,128)}) %all-reduce.4.cloned.1.call-update) | async-done | bytes 3538960
  1339.7 0.0 copy-done.1
  1339.7 2.1 fusion.26
  1341.8 0.0 all-gather.8.cloned.1.call-update
  1341.8 0.0 reduce-scatter.2.cloned.1.call-start
  1341.9 215.0 %all-gather.8.cloned.1.call-done = bf16[128,3,2304]{2,1,0:T(4,128)(2,1)} async-done(((bf16[1,3,2304]{2,1,0:T(4,128)(2,1)}), bf16[128,3,2304]{2,1,0:T(4,128)(2,1)}) %all-gather.8.cloned.1.call-update) | async-done | bytes 1769488 | tf_op jit(solution)/shard_map/all_gather | solution.py:35
  1556.9 4.1 reshape.20
  1561.0 1.6 convolution_bitcast_fusion.1
  1562.5 0.0 reduce-scatter.2.cloned.1.call-update
  1562.5 0.6 broadcast_multiply_fusion
  1563.2 100.5 %all-reduce.1 = (f32[]{:T(128)}, f32[]{:T(128)}) all-reduce(f32[]{:T(128)} %get-tuple-element.25, f32[]{:T(128)} %get-tuple-element.27), channel_id=1, replica_groups=mesh['feat'=128,'layer'=4] {'feat','layer'}, use_global_device_ids=true, to_apply=%region_2.3 | all-reduce | flops 2 | bytes 16 | tf_op jit(solution)/shard_map/psum | solution.py:37
  1664.9 1.5 fusion.25
  1666.5 1.8 fusion
  1668.3 0.0 reduce-scatter.2.cloned.1.call-done
  1668.3 3.3 fusion.1
Async XLA Ops:
  7.2 242.9 %copy-start = (bf16[4,1,64,2304]{3,2,1,0:T(8,128)(2,1)S(1)}, bf16[4,1,64,2304]{3,2,1,0:T(8,128)(2,1)}, u32[]{:S(2)}) copy-start(bf16[4,1,64,2304]{3,2,1,0:T(8,128)(2,1)} %param.8) | copy-start | bytes 3538948
  7.2 225.6 %all-gather.6.cloned.1.call-start = ((), (), s32[]{:S(2)}) async-start(), calls=%async_computation.2 | async-start | bytes 3566592 | tf_op jit(solution)/shard_map/all_gather | solution.py:15
  8.7 1331.0 %all-reduce.4.cloned.1.call-start = ((), (), s32[]{:S(2)}) async-start(), calls=%async_computation.4 | async-start | bytes 7077888
  252.6 1087.1 %copy-start.1 = (bf16[1,3,2304]{2,1,0:T(4,128)(2,1)S(1)}, bf16[1,3,2304]{2,1,0:T(4,128)(2,1)}, u32[]{:S(2)}) copy-start(bf16[1,3,2304]{2,1,0:T(4,128)(2,1)} %param.9) | copy-start | bytes 41476
  252.6 1304.3 %all-gather.8.cloned.1.call-start = ((), (), s32[]{:S(2)}) async-start(), calls=%async_computation.3 | async-start | bytes 2377728 | tf_op jit(solution)/shard_map/all_gather | solution.py:35
  1341.8 326.4 %reduce-scatter.2.cloned.1.call-start = ((), (), s32[]{:S(2)}) async-start(), calls=%async_computation.1 | async-start | bytes 491520 | tf_op jit(solution)/shard_map/reduce_scatter | solution.py:42
Sparse Core Ops, SparseCore 0:
  10.7 222.0 all-gather.5
  252.7 1086.9 all-reduce.3
  1342.4 214.4 all-gather.7
  1562.7 29.0 reduce-scatter.1
where the time goes:
time: 1680 us
  waiting for transfers between devices  1520 us (90%)
  blocking collectives  115 us (7%)
  between operations  16.9 us (1%)
    unnamed x5, waiting for transfers between devices  1090 us
    all_gather x1, waiting for transfers between devices, body(): lax.all_gather(local_rows, 'feat', axis=0, tiled=True)  223 us
    all_gather x1, waiting for transfers between devices, body(): grad_all = lax.all_gather(grad_local, 'feat', axis=0, tiled=True)  215 us
    psum x1, blocking collectives, body(): squares_total = lax.psum(squares_local, ('feat', 'layer'))  100 us
  transfers between devices with their start and end apart: 4, of which 3 were waited for; matrix products, arithmetic and copies ran while one was open for 0% of the time, Pallas kernels for 0%

commit v1 on v0

--- a/solution.py
+++ b/solution.py
@@ -1,3 +1,4 @@
+import functools
 import jax
 import jax.numpy as jnp
 from jax import lax
@@ -5,6 +6,21 @@
 
 ERROR_SCALE = 32.0
 PENALTY_WEIGHT = 4.0
+
+
+def register_things_up(load, k_dim):
+    return jnp.concatenate(
+        lax.all_to_all(
+            jnp.stack([load for _ in range(lax.axis_size("feat"))], axis=0),
+            axis_name="feat",
+            split_axis=0,
+            concat_axis=0,
+        ),
+        k_dim,
+    )
+
+
+set_the_slices = functools.partial(register_things_up, k_dim=0)
 
 
 def body(residual_in, enc_weight, thresholds, dec_weight, target):
@@ -32,7 +48,7 @@
     )
     error_rows = recon - target[0].astype(jnp.float32)
     grad_local = (error_rows / ERROR_SCALE).astype(jnp.bfloat16)
-    grad_all = lax.all_gather(grad_local, "feat", axis=0, tiled=True)
+    grad_all = set_the_slices(grad_local)
     squares_local = jnp.sum(error_rows * error_rows)
     squares_total = lax.psum(squares_local, ("feat", "layer"))
     dec_grad = jnp.einsum(

time: 1680 us -> 1530 us (0.911)
  waiting for transfers between devices: 1520 us -> 1310 us
  blocking collectives: 115 us -> 178 us
    all_gather x1 -> x0, waiting for transfers between devices: 215 us -> none  [body(): grad_all = lax.all_gather(grad_local, 'feat', axis=0, tiled=True)]
    all_to_all x0 -> x1, blocking collectives: none -> 64.9 us  [register_things_up(): lax.all_to_all(jnp.stack([load for _ in range(lax.axis_size('feat'))], ax...]
    unnamed x5 -> x4, waiting for transfers between devices: 1090 us -> 1090 us
  transfers between devices with their start and end apart: 4 -> 3, of which waited for: 3 -> 2; matrix products, arithmetic and copies ran while one was open for 0% -> 0% of each run, Pallas kernels for 0% -> 0%
where the time goes in v1:
time: 1530 us
  waiting for transfers between devices  1310 us (86%)
  blocking collectives  178 us (12%)
  between operations  16.9 us (1%)
    unnamed x4, waiting for transfers between devices  1090 us
    all_gather x1, waiting for transfers between devices, body(): lax.all_gather(local_rows, 'feat', axis=0, tiled=True)  223 us
    psum x1, blocking collectives, body(): squares_total = lax.psum(squares_local, ('feat', 'layer'))  99.1 us
    all_to_all x1, blocking collectives, register_things_up(): lax.all_to_all(jnp.stack([load for _ in range(lax.axis_size('feat'))], ax...  64.9 us
  transfers between devices with their start and end apart: 3, of which 2 were waited for; matrix products, arithmetic and copies ran while one was open for 0% of the time, Pallas kernels for 0%

profile of v1, /device:TPU:1, one launch (start us, length us, event | category | flops | bytes accessed | tf_op | source)
XLA Modules:
  0.0 1529.8 jit_solution(8850414569808949374)
XLA Ops:
  7.2 0.0 copy-start
  7.2 0.0 all-gather.4.cloned.1.call-start
  7.2 1.4 copy.19
  8.7 0.0 all-gather.4.cloned.1.call-update
  8.7 0.0 all-reduce.4.cloned.1.call-start
  8.7 0.7 multiply_bitcast_fusion
  9.4 223.4 %all-gather.4.cloned.1.call-done = bf16[1,384,2304]{2,0,1:T(2,128)(2,1)} async-done(((bf16[1,3,2304]{2,0,1:T(2,128)(2,1)}), bf16[1,384,2304]{2,0,1:T(2,128)(2,1)}) %all-gather.4.cloned.1.call-update) | async-done | bytes 1769488 | tf_op jit(solution)/shard_map/all_gather | solution.py:31
  232.8 3.4 fusion.14
  236.3 0.0 copy-start.4
  236.3 0.6 copy-done.4
  236.9 14.4 all-gather.1
  251.3 0.0 copy-start.2
  251.3 0.7 copy-done.2
  252.0 0.0 copy-done
  252.0 2.5 convolution_bitcast_fusion
  254.5 0.0 copy-start.7
  254.5 0.0 all-reduce.4.cloned.1.call-update
  254.5 0.0 reduce-scatter.2.cloned.1.call-start
  254.6 1.3 dynamic-slice
  256.5 1085.1 %all-reduce.4.cloned.1.call-done = f32[384,2304]{1,0:T(8,128)} async-done(((f32[384,2304]{1,0:T(8,128)}), f32[384,2304]{1,0:T(8,128)}) %all-reduce.4.cloned.1.call-update) | async-done | bytes 3538960
  1341.6 0.0 copy-done.7
  1341.6 1.5 multiply_convert_fusion
  1343.1 0.6 stack.2
  1343.8 64.9 %all_to_all.5 = bf16[128,3,2304]{2,1,0:T(4,128)(2,1)S(1)} all-to-all(bf16[128,3,2304]{2,1,0:T(4,128)(2,1)S(1)} %stack.2), channel_id=1, replica_groups=mesh['feat'=128,'layer'=4] {'feat'}, dimensions={0} | all-to-all | bytes 3538944 | tf_op jit(solution)/shard_map/all_to_all | solution.py:13
  1408.6 2.7 reshape.24
  1411.3 0.0 copy-start.1
  1411.3 0.0 copy-start.3
  1411.3 3.2 convolution_bitcast_fusion.1
  1414.5 0.0 copy-start.5
  1414.5 0.0 copy-start.6
  1414.5 0.0 reduce-scatter.2.cloned.1.call-update
  1414.6 0.6 broadcast_multiply_fusion
  1415.2 99.1 %all-reduce.1 = (f32[]{:T(128)}, f32[]{:T(128)}) all-reduce(f32[]{:T(128)} %get-tuple-element.25, f32[]{:T(128)} %get-tuple-element.27), channel_id=1, replica_groups=mesh['feat'=128,'layer'=4] {'feat','layer'}, use_global_device_ids=true, to_apply=%region_2.3 | all-reduce | flops 2 | bytes 16 | tf_op jit(solution)/shard_map/psum | solution.py:53
  1515.5 1.5 fusion.25
  1517.1 0.0 copy-done.1
  1517.1 0.0 copy-done.3
  1517.1 1.8 fusion
  1518.9 0.0 reduce-scatter.2.cloned.1.call-done
  1518.9 0.0 copy-done.5
  1518.9 0.0 copy-done.6
  1518.9 3.3 fusion.1
Async XLA Ops:
  7.2 244.8 %copy-start = (bf16[4,1,64,2304]{3,2,1,0:T(8,128)(2,1)S(1)}, bf16[4,1,64,2304]{3,2,1,0:T(8,128)(2,1)}, u32[]{:S(2)}) copy-start(bf16[4,1,64,2304]{3,2,1,0:T(8,128)(2,1)} %param.8) | copy-start | bytes 3538948
  7.2 225.6 %all-gather.4.cloned.1.call-start = ((), (), s32[]{:S(2)}) async-start(), calls=%async_computation.3 | async-start | bytes 3566592 | tf_op jit(solution)/shard_map/all_gather | solution.py:31
  8.7 1332.9 %all-reduce.4.cloned.1.call-start = ((), (), s32[]{:S(2)}) async-start(), calls=%async_computation.4 | async-start | bytes 7077888
  236.3 0.6 copy-start.4
  251.3 0.7 copy-start.2
  254.5 1087.1 %copy-start.7 = (bf16[1,3,2304]{2,1,0:T(4,128)(2,1)S(1)}, bf16[1,3,2304]{2,1,0:T(4,128)(2,1)}, u32[]{:S(2)}) copy-start(bf16[1,3,2304]{2,1,0:T(4,128)(2,1)} %param.9) | copy-start | bytes 41476
  254.5 1264.4 %reduce-scatter.2.cloned.1.call-start = ((), (), s32[]{:S(2)}) async-start(), calls=%async_computation.2 | async-start | bytes 491520 | tf_op jit(solution)/shard_map/reduce_scatter | solution.py:58
  1411.3 105.8 %copy-start.1 = (bf16[384,2304,1]{1,0,2:T(8,128)(2,1)S(1)}, bf16[384,2304,1]{1,0,2:T(8,128)(2,1)}, u32[]{:S(2)}) copy-start(bf16[384,2304,1]{1,0,2:T(8,128)(2,1)} %reshape.24) | copy-start | bytes 5308420
  1411.3 105.8 %copy-start.3 = (bf16[1536,64]{0,1:T(8,128)(2,1)S(1)}, bf16[1536,64]{0,1:T(8,128)(2,1)}, u32[]{:S(2)}) copy-start(bf16[1536,64]{0,1:T(8,128)(2,1)} %copy-done.2) | copy-start | bytes 589828
  1414.5 104.3 %copy-start.5 = (bf16[384,64]{0,1:T(8,128)(2,1)S(1)}, bf16[384,64]{0,1:T(8,128)(2,1)}, u32[]{:S(2)}) copy-start(bf16[384,64]{0,1:T(8,128)(2,1)} %copy-done.4) | copy-start | bytes 147460
  1414.5 104.3 %copy-start.6 = (f32[384,64]{0,1:T(8,128)S(1)}, f32[384,64]{0,1:T(8,128)}, u32[]{:S(2)}) copy-start(f32[384,64]{0,1:T(8,128)} %get-tuple-element.28) | copy-start | bytes 294916
Sparse Core Ops, SparseCore 0:
  10.7 222.0 all-gather.3
  254.6 1086.9 all-reduce.3
  1414.7 25.4 reduce-scatter.1
